TPU v7x, 128 devices: a whole 4x4x4 slice. The times are simulated.
128 devices in a mesh: row: 16 (over y, z), col: 8 (over x, core).
Axes of the slice: x: 4, y: 4, z: 4, core: 2. Of those that a mesh axis runs over, the one named last changes fastest.
Arguments:
- saved_inputs: bfloat16 [32768, 4096], P(('row', 'col')), may hold values from -6 to 6
- output_grads: bfloat16 [32768, 14336], P(('row', 'col')), may hold values from -0.5 to 0.5
- proj_in: bfloat16 [4096, 128], replicated, may hold values from -0.09375 to 0.09375
- proj_out: bfloat16 [14336, 128], replicated, may hold values from -0.046875 to 0.046875
- doc_lengths: int32 [128], replicated, may hold values from 64 to 448, as said below
- device_docs: int32 [128], replicated, may hold values from 0 to 127, as said below
- fisher_inverse: float32 [16384, 16384], P('row', 'col'), may hold values from -0.3 to 2.3, as said below
Outputs:
- preconditioned: float32 [128, 16384], P('row', 'col')
Inputs may be any that keep to these rules, and one draw needn't show every extreme that they name: `doc_lengths`: the lengths sum to 32768; some document has exactly 448 tokens and some exactly 64. `device_docs`: A permutation of the documents. `fisher_inverse`: Symmetric.
All inputs are finite; a program needn't handle non-finite values.
Results may differ from a plain program's by a relative error of at most 0.0041.
Values sent between devices are 32-bit elements; how exact they have to be, the bound alone decides.
A program may use at most 128 MiB of HBM per device.

v0:
```python
import jax
import jax.numpy as jnp
from jax import lax
from jax.sharding import PartitionSpec as P

SLOTS = 5


def per_device(
    saved_inputs, output_grads, proj_in, proj_out, doc_lengths, device_docs, fisher_inverse
):
    tok_count = saved_inputs.shape[0]
    n_row = lax.axis_size("row")
    n_col = lax.axis_size("col")
    doc_count = doc_lengths.shape[0]
    rank_in = proj_in.shape[1]
    rank_out = proj_out.shape[1]
    feat_count = rank_in * rank_out
    block_width = feat_count // n_row
    shard_index = lax.axis_index("row") * n_col + lax.axis_index("col")
    low_in = jnp.dot(saved_inputs, proj_in, preferred_element_type=jnp.float32).astype(jnp.bfloat16)
    low_out = jnp.dot(output_grads, proj_out, preferred_element_type=jnp.float32).astype(
        jnp.bfloat16
    )
    doc_ends = jnp.cumsum(doc_lengths)
    starts = doc_ends - doc_lengths
    positions = shard_index * tok_count + jnp.arange(tok_count, dtype=jnp.int32)
    doc_ids = jnp.sum((starts[None, :] <= positions[:, None]).astype(jnp.int32), axis=1) - 1
    first_doc = doc_ids[0]
    slot_range = jnp.arange(SLOTS, dtype=jnp.int32)
    slot_masks = (doc_ids[:, None] - first_doc == slot_range[None, :]).astype(jnp.bfloat16)
    masked = (slot_masks[:, :, None] * low_out[:, None, :]).reshape(tok_count, SLOTS * rank_out)
    partials = lax.dot_general(
        masked, low_in, (((0,), (0,)), ((), ())), preferred_element_type=jnp.float32
    )
    partials = partials.reshape(SLOTS, feat_count)
    placer = (device_docs[:, None] == (first_doc + slot_range)[None, :]).astype(jnp.float32)
    dense_sums = jnp.dot(
        placer, partials, precision=lax.Precision.HIGHEST, preferred_element_type=jnp.float32
    )
    own_docs = lax.psum_scatter(dense_sums, ("row", "col"), scatter_dimension=0, tiled=True)
    docs_dev = own_docs.shape[0]
    spread = lax.all_to_all(own_docs, "row", split_axis=1, concat_axis=0, tiled=True)
    gathered = lax.all_gather(spread, "col", axis=0, tiled=True)
    doc_block = gathered.reshape(n_col, n_row, docs_dev, block_width)
    doc_block = doc_block.transpose(1, 0, 2, 3).reshape(doc_count, block_width)
    return lax.psum_scatter(
        jnp.dot(
            doc_block,
            fisher_inverse,
            precision=lax.Precision.HIGHEST,
            preferred_element_type=jnp.float32,
        ),
        "row",
        scatter_dimension=0,
        tiled=True,
    )


def solution(mesh):
    placed = (P(("row", "col"), None), P(("row", "col"), None), P(), P(), P(), P(), P("row", "col"))
    return jax.shard_map(
        per_device, mesh=mesh, in_specs=placed, out_specs=P("row", "col"), check_vma=False
    )
```

profile of v0, /device:TPU:1, one launch (start us, length us, event | category | flops | bytes accessed | tf_op | source)
XLA Modules:
  0.0 315.2 jit_solution(14136184809416230603)
XLA Ops:
  6.5 0.0 copy-start
  6.5 0.0 all-reduce.5.cloned.1.call-start
  6.5 0.9 copy.19
  7.5 0.2 reduce-window.9
  7.6 0.1 reduce
  7.7 0.7 sub.18
  8.4 0.2 convert_reduce_fusion
  8.6 0.5 slice.3
  9.1 0.6 broadcast_subtract_fusion
  9.8 0.7 iota_add_fusion.1
  10.4 0.0 copy-start.1
  10.4 6.2 %convolution_convert_fusion.1 = bf16[256,128]{1,0:T(8,128)(2,1)S(1)} fusion(bf16[256,14336]{1,0:T(8,128)(2,1)} %param.8, bf16[14336,128]{1,0:T(8,128)(2,1)} %param.10), kind=kOutput, calls=%fused_computation.1 | convolution fusion | flops 939556864 | bytes 11075584 | tf_op jit(solution)/shard_map/dot_general | solution.py:22
  16.6 0.1 copy.20
  16.8 0.0 copy-done
  16.8 2.1 fusion
  18.9 0.1 reshape.84
  19.0 0.0 copy-done.1
  19.0 5.7 %fusion.4 = f32[128,16384]{1,0:T(8,128)} fusion(f32[5,16384]{1,0:T(8,128)S(1)} %reshape.84, s32[5]{0:T(128)S(1)} %iota_add_fusion.1, s32[128]{0:T(128)S(1)} %copy-done.1), kind=kOutput, calls=%fused_computation.8 | convolution fusion | flops 125829760 | bytes 8716820 | tf_op jit(solution)/shard_map/dot_general | solution.py:38
  24.7 0.0 all-reduce.5.cloned.1.call-update
  24.7 0.0 copy-start.2
  24.7 0.0 all-reduce.7.cloned.1.call-start
  24.8 164.9 %all-reduce.5.cloned.1.call-done = f32[128,16384]{1,0:T(8,128)} async-done(((f32[128,16384]{1,0:T(8,128)}), f32[128,16384]{1,0:T(8,128)}) %all-reduce.5.cloned.1.call-update) | async-done | bytes 8388624
  189.7 1.1 constant_dynamic-slice_fusion.1
  190.8 11.6 %all_to_all.16 = f32[1,16,1024]{2,0,1:T(1,128)S(1)} all-to-all(f32[1,16,1024]{2,0,1:T(1,128)S(1)} %bitcast.20), channel_id=1, replica_groups=mesh['row'=16,'col'=8] {'row'}, dimensions={1} | all-to-all | bytes 131072 | tf_op jit(solution)/shard_map/all_to_all | solution.py:43
  202.4 14.8 %all-gather = f32[1,128,1024]{2,1,0:T(8,128)S(1)} all-gather(f32[1,16,1024]{2,1,0:T(8,128)S(1)} %copy.22), channel_id=2, replica_groups=mesh['row'=16,'col'=8] {'col'}, dimensions={1}, use_global_device_ids=true | all-gather | bytes 589824 | tf_op jit(solution)/shard_map/all_gather | solution.py:44
  217.3 8.0 %fusion.1 = f32[128,2048]{1,0:T(8,128)} fusion(f32[1024,2048]{1,0:T(8,128)} %param.13, f32[16,8,1,1024]{3,0,1,2:T(8,128)S(1)} %bitcast.18), kind=kOutput, calls=%fused_computation.3 | convolution fusion | flops 3221225472 | bytes 9961472 | tf_op jit(solution)/shard_map/dot_general | solution.py:48
  225.3 0.0 all-reduce.7.cloned.1.call-update
  225.3 0.0 copy-done.2
  225.3 0.6 dynamic-slice.1
  226.5 80.4 %all-reduce.7.cloned.1.call-done = f32[128,2048]{1,0:T(8,128)} async-done(((f32[128,2048]{1,0:T(8,128)}), f32[128,2048]{1,0:T(8,128)}) %all-reduce.7.cloned.1.call-update) | async-done | bytes 1048592
  306.9 1.5 constant_dynamic-slice_fusion
  (5 shorter events, 0.1 us)
Async XLA Ops:
  6.5 10.3 %copy-start = (bf16[256,4096]{1,0:T(8,128)(2,1)S(1)}, bf16[256,4096]{1,0:T(8,128)(2,1)}, u32[]{:S(2)}) copy-start(bf16[256,4096]{1,0:T(8,128)(2,1)} %param.7) | copy-start | bytes 6291460
  6.5 183.2 %all-reduce.5.cloned.1.call-start = ((), (), s32[]{:S(2)}) async-start(), calls=%async_computation.1 | async-start | bytes 16777216
  10.4 8.6 %copy-start.1 = (s32[128]{0:T(128)S(1)}, s32[128]{0:T(128)}, u32[]{:S(2)}) copy-start(s32[128]{0:T(128)} %param.12) | copy-start | bytes 1540
  24.7 200.6 %copy-start.2 = (u32[128]{0:T(128)S(1)}, u32[128]{0:T(128)}, u32[]{:S(2)}) copy-start(u32[128]{0:T(128)} %constant.26) | copy-start | bytes 1540
  24.7 282.2 %all-reduce.7.cloned.1.call-start = ((), (), s32[]{:S(2)}) async-start(), calls=%async_computation.2 | async-start | bytes 2097152
Sparse Core Ops, SparseCore 0:
  24.8 164.8 all-reduce.4
  225.4 81.4 all-reduce.6
where the time goes:
time: 316 us; the launch traced here: 315 us
  waiting for transfers between devices  245 us (78%)
  blocking collectives  26.4 us (8%)
  matrix products  22 us (7%)
  between operations  14.2 us (4%)
  local copies, waits for them, and re-layouts  4.8 us (2%)
    unnamed x4, waiting for transfers between devices  245 us
    all_gather x1, blocking collectives, per_device(): gathered = lax.all_gather(spread, 'col', axis=0, tiled=True)  14.8 us
    all_to_all x1, blocking collectives, per_device(): lax.all_to_all(own_docs, 'row', split_axis=1, concat_axis=0, tiled=True)  11.6 us
    dot_general x1, matrix products, per_device(): jnp.dot(doc_block, fisher_inverse, precision=lax.Precision.HIGHEST, prefe...  8.01 us
  transfers between devices with their start and end apart: 2, of which 2 were waited for; matrix products, arithmetic and copies ran while one was open for 0% of the time, Pallas kernels for 0%

commit v1 on v0

v1 whole, which is shorter than its diff:
```python
import jax
import jax.numpy as jnp
from jax import lax
from jax.experimental import pallas as pl
from jax.experimental.pallas import tpu as pltpu
from jax.sharding import PartitionSpec as P

SLOTS = 5
F32 = jnp.float32
BF16 = jnp.bfloat16
MESH = pl.DeviceIdType.MESH


def split(x):
    hi = x.astype(BF16)
    return hi, (x - hi.astype(F32)).astype(BF16)


def dot(a, b):
    return jnp.dot(a, b, preferred_element_type=F32)


def body(
    chunk, si, og, pi, po, dl, dd, fi, out,
    x, w, f32buf, fhi, flo, sel, pbuf, rbuf, sbuf, tbuf, gbuf, ybuf, obuf,
    x_sem, w_sem, f_sem, s1, r1, s2, r2, s3, r3, s4, r4,
):
    n_row = lax.axis_size("row")
    n_col = lax.axis_size("col")
    row = lax.axis_index("row")
    col = lax.axis_index("col")
    tok, d_in = si.shape
    rank = pi.shape[1]
    docs = dl.shape[1]
    n_in = d_in // chunk
    n_all = n_in + og.shape[1] // chunk
    piece = SLOTS * n_col
    lot = SLOTS * n_row

    loads = []
    for k in range(n_all):
        a, b, i = (si, pi, k) if k < n_in else (og, po, k - n_in)
        cols = pl.ds(i * chunk, chunk)
        loads.append((
            pltpu.make_async_copy(a.at[:, cols], x.at[k], x_sem.at[k]),
            pltpu.make_async_copy(b.at[cols, :], w.at[k], w_sem.at[k]),
        ))
        for c in loads[-1]:
            c.start()
    f_load = pltpu.make_async_copy(fi, f32buf, f_sem)
    f_load.start()

    barrier = pltpu.get_barrier_semaphore()

    @pl.loop(1, n_row)
    def _(j):
        pl.semaphore_signal(barrier, inc=1, device_id={"row": lax.rem(row + j, n_row), "col": col}, device_id_type=MESH)

    @pl.loop(1, n_col)
    def _(j):
        pl.semaphore_signal(barrier, inc=1, device_id={"row": row, "col": lax.rem(col + j, n_col)}, device_id_type=MESH)

    lens = jnp.broadcast_to(dl[...].astype(F32), (docs, docs))
    down = lax.broadcasted_iota(jnp.int32, (docs, docs), 0)
    along = lax.broadcasted_iota(jnp.int32, (docs, docs), 1)
    starts_col = jnp.sum(jnp.where(along < down, lens, 0.0), axis=1, keepdims=True)
    starts_row = jnp.sum(jnp.where(down == along, starts_col, 0.0), axis=0, keepdims=True)
    owner_col = jnp.sum(jnp.where(down == along, dd[...].astype(F32), 0.0), axis=1, keepdims=True)

    lanes = lax.broadcasted_iota(jnp.int32, (1, n_col * lot), 1)
    shard = lax.rem(lanes, lot) // SLOTS * n_col + lanes // lot
    first = jnp.sum(jnp.where(starts_col <= (shard * tok).astype(F32), 1.0, 0.0), axis=0, keepdims=True) - 1.0
    slot_doc = first + lax.rem(lanes, SLOTS).astype(F32)
    sel[...] = jnp.where(owner_col == slot_doc, 1.0, 0.0).astype(BF16)

    base = (row * n_col + col) * tok
    pos = base + lax.broadcasted_iota(jnp.int32, (tok, 1), 0)
    begun = (starts_row <= pos.astype(F32)) & (starts_row > jnp.full((1, 1), base, jnp.int32).astype(F32))
    slot = jnp.sum(jnp.where(begun, 1.0, 0.0), axis=1, keepdims=True)

    low = []
    for lo, hi in ((0, n_in), (n_in, n_all)):
        acc = None
        for k in range(lo, hi):
            for c in loads[k]:
                c.wait()
            term = dot(x[k], w[k])
            acc = term if acc is None else acc + term
        low.append(acc.astype(BF16))
    low_in, low_out = low
    masked = jnp.concatenate(
        [jnp.where(slot == float(s), low_in, jnp.zeros_like(low_in)) for s in range(SLOTS)], axis=1
    )
    part = lax.dot_general(low_out, masked, (((0,), (0,)), ((), ())), preferred_element_type=F32)
    for r in range(n_row):
        for s in range(SLOTS):
            pbuf[pl.ds(r * piece + s * n_col, n_col), :] = part[r * n_col:(r + 1) * n_col, s * rank:(s + 1) * rank]

    pl.semaphore_wait(barrier, n_row + n_col - 2)

    def over_row(src, dst, send, recv, j, step):
        to = lax.rem(row + j, n_row)
        return pltpu.make_async_remote_copy(
            src_ref=src.at[pl.ds(to * step, step), :], dst_ref=dst.at[pl.ds(row * step, step), :],
            send_sem=send.at[j], recv_sem=recv.at[j], device_id={"row": to, "col": col}, device_id_type=MESH,
        )

    def over_col(src, dst, send, recv, j, step, whole):
        to = lax.rem(col + j, n_col)
        at = col if whole else to
        return pltpu.make_async_remote_copy(
            src_ref=src.at[pl.ds(at * step, step), :], dst_ref=dst.at[pl.ds(col * step, step), :],
            send_sem=send.at[j], recv_sem=recv.at[j], device_id={"row": row, "col": to}, device_id_type=MESH,
        )

    @pl.loop(1, n_row)
    def _(j):
        over_row(pbuf, rbuf, s1, r1, j, piece).start()

    rbuf[pl.ds(row * piece, piece), :] = pbuf[pl.ds(row * piece, piece), :]

    f_load.wait()

    @pl.loop(0, fi.shape[0] // 32)
    def _(i):
        at = pl.ds(pl.multiple_of(i * 32, 32), 32)
        fhi[at, :], flo[at, :] = split(f32buf[at, :])

    @pl.loop(1, n_row)
    def _(j):
        over_row(pbuf, rbuf, s1, r1, j, piece).wait()

    for c in range(n_col):
        sbuf[pl.ds(c * lot, lot), :] = rbuf[pl.ds(c, lot, stride=n_col), :]

    @pl.loop(1, n_col)
    def _(j):
        over_col(sbuf, tbuf, s2, r2, j, lot, False).start()

    tbuf[pl.ds(col * lot, lot), :] = sbuf[pl.ds(col * lot, lot), :]

    @pl.loop(1, n_col)
    def _(j):
        over_col(sbuf, tbuf, s2, r2, j, lot, False).wait()

    t_hi, t_lo = split(tbuf[...])
    gbuf[pl.ds(col * docs, docs), :] = dot(sel[...], t_hi) + dot(sel[...], t_lo)

    @pl.loop(1, n_col)
    def _(j):
        over_col(gbuf, gbuf, s3, r3, j, docs, True).start()

    @pl.loop(1, n_col)
    def _(j):
        over_col(gbuf, gbuf, s3, r3, j, docs, True).wait()

    g = jnp.concatenate([gbuf[c * docs:(c + 1) * docs, :] for c in range(n_col)], axis=1)
    g_hi, g_lo = split(g)

    @pl.loop(0, ybuf.shape[1] // 256)
    def _(n):
        at = pl.ds(pl.multiple_of(n * 256, 256), 256)
        ybuf[:, at] = dot(g_hi, fhi[:, at]) + (dot(g_hi, flo[:, at]) + dot(g_lo, fhi[:, at]))

    rows = docs // n_row

    @pl.loop(1, n_row)
    def _(j):
        over_row(ybuf, obuf, s4, r4, j, rows).start()

    obuf[pl.ds(row * rows, rows), :] = ybuf[pl.ds(row * rows, rows), :]

    @pl.loop(1, n_row)
    def _(j):
        over_row(ybuf, obuf, s4, r4, j, rows).wait()

    total = obuf[0:rows, :]
    for r in range(1, n_row):
        total = total + obuf[r * rows:(r + 1) * rows, :]
    out[...] = total


def per_device(saved_inputs, output_grads, proj_in, proj_out, doc_lengths, device_docs, fisher_inverse):
    n_row, n_col = lax.axis_size("row"), lax.axis_size("col")
    tok, d_in = saved_inputs.shape
    ff = output_grads.shape[1]
    rank = proj_in.shape[1]
    docs = doc_lengths.shape[0]
    feats, cols = fisher_inverse.shape
    chunk = 2048
    n_all = (d_in + ff) // chunk
    slots = n_row * n_col * SLOTS
    dma = pltpu.SemaphoreType.DMA
    hbm = pl.BlockSpec(memory_space=pl.ANY)
    vmem = pl.BlockSpec(memory_space=pltpu.VMEM)

    def kernel(*refs):
        body(chunk, *refs)

    return pl.pallas_call(
        kernel,
        out_shape=jax.ShapeDtypeStruct((docs // n_row, cols), F32),
        in_specs=[hbm, hbm, hbm, hbm, vmem, vmem, hbm],
        out_specs=vmem,
        scratch_shapes=[
            pltpu.VMEM((n_all, tok, chunk), BF16),
            pltpu.VMEM((n_all, chunk, rank), BF16),
            pltpu.VMEM((feats, cols), F32),
            pltpu.VMEM((feats, cols), BF16),
            pltpu.VMEM((feats, cols), BF16),
            pltpu.VMEM((docs, slots), BF16),
            pltpu.VMEM((slots, rank), F32),
            pltpu.VMEM((slots, rank), F32),
            pltpu.VMEM((slots, rank), F32),
            pltpu.VMEM((slots, rank), F32),
            pltpu.VMEM((n_col * docs, rank), F32),
            pltpu.VMEM((docs, cols), F32),
            pltpu.VMEM((docs, cols), F32),
            dma((n_all,)), dma((n_all,)), dma,
            dma((n_row,)), dma((n_row,)), dma((n_col,)), dma((n_col,)),
            dma((n_col,)), dma((n_col,)), dma((n_row,)), dma((n_row,)),
        ],
        compiler_params=pltpu.CompilerParams(
            collective_id=0, has_side_effects=True, vmem_limit_bytes=56 << 20
        ),
    )(
        saved_inputs, output_grads, proj_in, proj_out,
        doc_lengths.reshape(1, docs), device_docs.reshape(1, docs), fisher_inverse,
    )


def solution(mesh):
    placed = (P(("row", "col"), None), P(("row", "col"), None), P(), P(), P(), P(), P("row", "col"))
    return jax.shard_map(
        per_device, mesh=mesh, in_specs=placed, out_specs=P("row", "col"), check_vma=False
    )
```

time: 316 us -> 53.2 us (0.17)
  waiting for transfers between devices: 245 us -> 0 us
  Pallas kernels: 0 us -> 51.3 us
  blocking collectives: 26.4 us -> 0 us
  matrix products: 22 us -> 0 us
  between operations: 14.2 us -> 0.01 us
  local copies, waits for them, and re-layouts: 4.8 us -> 1.47 us
    unnamed x4 -> x0, waiting for transfers between devices: 245 us -> none
    pallas_call x0 -> x1, Pallas kernels: none -> 51.3 us  [per_device(): pl.pallas_call(kernel, out_shape=jax.ShapeDtypeStruct((docs // n_row, col...]
    dot_general x4 -> x0, matrix products: 22 us -> none  [the longest x1 8.01 us: per_device(): jnp.dot(doc_block, fisher_inverse, precision=lax.Precision.HIGHEST, prefe...]
    all_gather x1 -> x0, blocking collectives: 14.8 us -> none  [per_device(): gathered = lax.all_gather(spread, 'col', axis=0, tiled=True)]
    all_to_all x1 -> x0, blocking collectives: 11.6 us -> none  [per_device(): lax.all_to_all(own_docs, 'row', split_axis=1, concat_axis=0, tiled=True)]
  transfers between devices with their start and end apart: 2 -> 0, of which waited for: 2 -> 0; matrix products, arithmetic and copies ran while one was open for 0% -> 0% of each run, Pallas kernels for 0% -> 0%
where the time goes in v1:
time: 53.2 us; the launch traced here: 52.8 us
  Pallas kernels  51.3 us (96%)
  local copies, waits for them, and re-layouts  1.47 us (3%)
    pallas_call x1, Pallas kernels, per_device(): pl.pallas_call(kernel, out_shape=jax.ShapeDtypeStruct((docs // n_row, col...  51.3 us
    unnamed x1, local copies, waits for them, and re-layouts  1.47 us

profile of v1, /device:TPU:1, one launch (start us, length us, event | category | flops | bytes accessed | tf_op | source)
XLA Modules:
  0.0 52.8 jit_solution(17886333776104747318)
XLA Ops:
  0.0 51.3 %shard_map.73 = f32[8,2048]{1,0:T(8,128)} custom-call(bf16[256,4096]{1,0:T(8,128)(2,1)} %refs_0_.1, bf16[256,14336]{1,0:T(8,128)(2,1)} %refs_1_.1, bf16[4096,128]{1,0:T(8,128)(2,1)} %refs_2_.1, bf16[14336,128]{1,0:T(8,128)(2,1)} %refs_3_.1, s32[1,128]{1,0:T(1,128)} %bitcast.2, s32[1,128]{1,0:T(1,128)} %bitcast.3, f32[1024,2048]{1,0:T(8,128)} %refs_6_.1), custom_call_target="tpu_custom_call" | custom-call | tf_op jit(solution)/shard_map/pallas_call | solution.py:200
  51.3 1.5 %copy.9 = f32[8,2048]{1,0:T(8,128)} copy(f32[8,2048]{1,0:T(8,128)} %shard_map.73) | data formatting | bytes 131072

commit v2 on v1

--- a/solution.py
+++ b/solution.py
@@ -6,6 +6,9 @@
 from jax.sharding import PartitionSpec as P
 
 SLOTS = 5
+CORES = 2
+NZ = 4
+CHUNKS = 4
 F32 = jnp.float32
 BF16 = jnp.bfloat16
 MESH = pl.DeviceIdType.MESH
@@ -22,8 +25,8 @@
 
 def body(
     chunk, si, og, pi, po, dl, dd, fi, out,
-    x, w, f32buf, fhi, flo, sel, pbuf, rbuf, sbuf, tbuf, gbuf, ybuf, obuf,
-    x_sem, w_sem, f_sem, s1, r1, s2, r2, s3, r3, s4, r4,
+    x, w, f32buf, fhi, flo, sel, pbuf, rbuf, sbuf, tbuf, gbuf, ghi, glo, ybuf, mbuf, qbuf, obuf,
+    x_sem, w_sem, f_sem, s1, r1, s2, r2, s3, r3, s5, r5, s4, r4, s6, r6,
 ):
     n_row = lax.axis_size("row")
     n_col = lax.axis_size("col")
@@ -144,40 +147,94 @@
         over_col(sbuf, tbuf, s2, r2, j, lot, False).wait()
 
     t_hi, t_lo = split(tbuf[...])
-    gbuf[pl.ds(col * docs, docs), :] = dot(sel[...], t_hi) + dot(sel[...], t_lo)
-
-    @pl.loop(1, n_col)
-    def _(j):
-        over_col(gbuf, gbuf, s3, r3, j, docs, True).start()
-
-    @pl.loop(1, n_col)
-    def _(j):
-        over_col(gbuf, gbuf, s3, r3, j, docs, True).wait()
-
-    g = jnp.concatenate([gbuf[c * docs:(c + 1) * docs, :] for c in range(n_col)], axis=1)
-    g_hi, g_lo = split(g)
-
-    @pl.loop(0, ybuf.shape[1] // 256)
-    def _(n):
-        at = pl.ds(pl.multiple_of(n * 256, 256), 256)
-        ybuf[:, at] = dot(g_hi, fhi[:, at]) + (dot(g_hi, flo[:, at]) + dot(g_lo, fhi[:, at]))
-
+    gbuf[col] = dot(sel[...], t_hi) + dot(sel[...], t_lo)
+
+    nx = n_col // CORES
+    cx = col // CORES
+    core = lax.rem(col, CORES)
+    sibling = col + 1 - 2 * core
+
+    def hand(at, to, send, recv):
+        return pltpu.make_async_remote_copy(
+            src_ref=gbuf.at[at], dst_ref=gbuf.at[at], send_sem=send, recv_sem=recv,
+            device_id={"row": row, "col": to}, device_id_type=MESH,
+        )
+
+    def keep(at):
+        ghi[at], glo[at] = split(gbuf[at])
+
+    around = [hand(col, lax.rem(cx + j, nx) * CORES + core, s3.at[j], r3.at[j]) for j in range(1, nx)]
+    across = [hand(col, sibling, s5.at[0], r5.at[0])]
+    for c in around + across:
+        c.start()
+    keep(col)
+    for j in range(1, nx):
+        around[j - 1].wait_recv()
+        at = lax.rem(cx + nx - j, nx) * CORES + core
+        across.append(hand(at, sibling, s5.at[j], r5.at[j]))
+        across[j].start()
+        keep(at)
+    for j in range(nx):
+        across[j].wait_recv()
+        keep(lax.rem(cx + nx - j, nx) * CORES + 1 - core)
+
+    ny = n_row // NZ
+    y, z = row // NZ, lax.rem(row, NZ)
     rows = docs // n_row
-
-    @pl.loop(1, n_row)
-    def _(j):
-        over_row(ybuf, obuf, s4, r4, j, rows).start()
-
-    obuf[pl.ds(row * rows, rows), :] = ybuf[pl.ds(row * rows, rows), :]
-
-    @pl.loop(1, n_row)
-    def _(j):
-        over_row(ybuf, obuf, s4, r4, j, rows).wait()
-
-    total = obuf[0:rows, :]
-    for r in range(1, n_row):
-        total = total + obuf[r * rows:(r + 1) * rows, :]
-    out[...] = total
+    wide = ybuf.shape[3] // CHUNKS
+    g_hi = jnp.concatenate([ghi[c] for c in range(n_col)], axis=1)
+    g_lo = jnp.concatenate([glo[c] for c in range(n_col)], axis=1)
+
+    def peer(along_y, j):
+        if along_y:
+            to = lax.rem(y + j, ny)
+            return to, {"row": to * NZ + z, "col": col}
+        to = lax.rem(z + j, NZ)
+        return to, {"row": y * NZ + to, "col": col}
+
+    first_hop, second_hop = [], []
+    for n in range(CHUNKS):
+        cols = slice(n * wide, (n + 1) * wide)
+        f_hi, f_lo = fhi[:, cols], flo[:, cols]
+        prod = dot(g_hi, f_hi) + (dot(g_hi, f_lo) + dot(g_lo, f_hi))
+        ybuf[:, :, :, cols] = prod.reshape(ny, NZ, rows, wide)
+        hops = []
+        for j in range(1, ny if n % 2 == 0 else NZ):
+            to, device = peer(n % 2 == 0, j)
+            src = ybuf.at[to, :, :, cols] if n % 2 == 0 else ybuf.at[:, to, :, cols]
+            hops.append(pltpu.make_async_remote_copy(
+                src_ref=src, dst_ref=mbuf.at[n, j - 1], send_sem=s4.at[n, j], recv_sem=r4.at[n, j],
+                device_id=device, device_id_type=MESH,
+            ))
+            hops[-1].start()
+        first_hop.append(hops)
+
+    for n in range(CHUNKS):
+        cols = slice(n * wide, (n + 1) * wide)
+        part = ybuf[y, :, :, cols] if n % 2 == 0 else ybuf[:, z, :, cols]
+        for j, c in enumerate(first_hop[n]):
+            c.wait_recv()
+            part = part + mbuf[n, j]
+        qbuf[n] = part
+        hops = []
+        for j in range(1, NZ if n % 2 == 0 else ny):
+            to, device = peer(n % 2 == 1, j)
+            hops.append(pltpu.make_async_remote_copy(
+                src_ref=qbuf.at[n, to], dst_ref=obuf.at[n, j - 1], send_sem=s6.at[n, j], recv_sem=r6.at[n, j],
+                device_id=device, device_id_type=MESH,
+            ))
+            hops[-1].start()
+        second_hop.append(hops)
+
+    for n in range(CHUNKS):
+        total = qbuf[n, z if n % 2 == 0 else y]
+        for j, c in enumerate(second_hop[n]):
+            c.wait_recv()
+            total = total + obuf[n, j]
+        out[:, n * wide:(n + 1) * wide] = total
+
+    for c in around + across + sum(first_hop + second_hop, []):
+        c.wait_send()
 
 
 def per_device(saved_inputs, output_grads, proj_in, proj_out, doc_lengths, device_docs, fisher_inverse):
@@ -190,6 +247,7 @@
     chunk = 2048
     n_all = (d_in + ff) // chunk
     slots = n_row * n_col * SLOTS
+    ny, nx, rows = n_row // NZ, n_col // CORES, docs // n_row
     dma = pltpu.SemaphoreType.DMA
     hbm = pl.BlockSpec(memory_space=pl.ANY)
     vmem = pl.BlockSpec(memory_space=pltpu.VMEM)
@@ -213,12 +271,17 @@
             pltpu.VMEM((slots, rank), F32),
             pltpu.VMEM((slots, rank), F32),
             pltpu.VMEM((slots, rank), F32),
-            pltpu.VMEM((n_col * docs, rank), F32),
-            pltpu.VMEM((docs, cols), F32),
-            pltpu.VMEM((docs, cols), F32),
+            pltpu.VMEM((n_col, docs, rank), F32),
+            pltpu.VMEM((n_col, docs, rank), BF16),
+            pltpu.VMEM((n_col, docs, rank), BF16),
+            pltpu.VMEM((ny, NZ, rows, cols), F32),
+            pltpu.VMEM((CHUNKS, NZ - 1, NZ, rows, cols // CHUNKS), F32),
+            pltpu.VMEM((CHUNKS, NZ, rows, cols // CHUNKS), F32),
+            pltpu.VMEM((CHUNKS, NZ - 1, rows, cols // CHUNKS), F32),
             dma((n_all,)), dma((n_all,)), dma,
             dma((n_row,)), dma((n_row,)), dma((n_col,)), dma((n_col,)),
-            dma((n_col,)), dma((n_col,)), dma((n_row,)), dma((n_row,)),
+            dma((nx,)), dma((nx,)), dma((nx,)), dma((nx,)),
+            dma((CHUNKS, NZ)), dma((CHUNKS, NZ)), dma((CHUNKS, NZ)), dma((CHUNKS, NZ)),
         ],
         compiler_params=pltpu.CompilerParams(
             collective_id=0, has_side_effects=True, vmem_limit_bytes=56 << 20

time: 53.2 us -> 46.5 us (0.87)
  Pallas kernels: 51.3 us -> 44.9 us
    pallas_call x1, Pallas kernels: 51.3 us -> 44.9 us  [per_device(): pl.pallas_call(kernel, out_shape=jax.ShapeDtypeStruct((docs // n_row, col...]
where the time goes in v2:
time: 46.5 us; the launch traced here: 46.3 us
  Pallas kernels  44.9 us (97%)
  local copies, waits for them, and re-layouts  1.47 us (3%)
    pallas_call x1, Pallas kernels, per_device(): pl.pallas_call(kernel, out_shape=jax.ShapeDtypeStruct((docs // n_row, col...  44.9 us
    unnamed x1, local copies, waits for them, and re-layouts  1.47 us

profile of v2, /device:TPU:1, one launch (start us, length us, event | category | flops | bytes accessed | tf_op | source)
XLA Modules:
  0.0 46.3 jit_solution(5179360781266093162)
XLA Ops:
  0.0 44.9 %shard_map.73 = f32[8,2048]{1,0:T(8,128)} custom-call(bf16[256,4096]{1,0:T(8,128)(2,1)} %refs_0_.1, bf16[256,14336]{1,0:T(8,128)(2,1)} %refs_1_.1, bf16[4096,128]{1,0:T(8,128)(2,1)} %refs_2_.1, bf16[14336,128]{1,0:T(8,128)(2,1)} %refs_3_.1, s32[1,128]{1,0:T(1,128)} %bitcast.2, s32[1,128]{1,0:T(1,128)} %bitcast.3, f32[1024,2048]{1,0:T(8,128)} %refs_6_.1), custom_call_target="tpu_custom_call" | custom-call | tf_op jit(solution)/shard_map/pallas_call | solution.py:258
  44.9 1.5 %copy.9 = f32[8,2048]{1,0:T(8,128)} copy(f32[8,2048]{1,0:T(8,128)} %shard_map.73) | data formatting | bytes 131072

commit v3 on v2

--- a/solution.py
+++ b/solution.py
@@ -6,6 +6,7 @@
 from jax.sharding import PartitionSpec as P
 
 SLOTS = 5
+PAD = 8
 CORES = 2
 NZ = 4
 CHUNKS = 4
@@ -25,8 +26,8 @@
 
 def body(
     chunk, si, og, pi, po, dl, dd, fi, out,
-    x, w, f32buf, fhi, flo, sel, pbuf, rbuf, sbuf, tbuf, gbuf, ghi, glo, ybuf, mbuf, qbuf, obuf,
-    x_sem, w_sem, f_sem, s1, r1, s2, r2, s3, r3, s5, r5, s4, r4, s6, r6,
+    x, w, f32buf, fhi, flo, sel, pbuf, tbuf, gbuf, ghi, glo, ybuf, mbuf, qbuf, obuf,
+    x_sem, w_sem, f_sem, s1, r1, s3, r3, s5, r5, s4, r4, s6, r6,
 ):
     n_row = lax.axis_size("row")
     n_col = lax.axis_size("col")
@@ -37,8 +38,20 @@
     docs = dl.shape[1]
     n_in = d_in // chunk
     n_all = n_in + og.shape[1] // chunk
-    piece = SLOTS * n_col
-    lot = SLOTS * n_row
+    n_dev = n_row * n_col
+    me = row * n_col + col
+
+    def each_other(act):
+        for lo, hi in ((n_row // 2, n_row), (1, n_row // 2)):
+            @pl.loop(lo, hi)
+            def _(j):
+                to = lax.rem(row + j, n_row)
+                for c in range(n_col):
+                    act(to, c)
+
+        @pl.loop(1, n_col)
+        def _(j):
+            act(row, lax.rem(col + j, n_col))
 
     loads = []
     for k in range(n_all):
@@ -55,13 +68,10 @@
 
     barrier = pltpu.get_barrier_semaphore()
 
-    @pl.loop(1, n_row)
-    def _(j):
-        pl.semaphore_signal(barrier, inc=1, device_id={"row": lax.rem(row + j, n_row), "col": col}, device_id_type=MESH)
-
-    @pl.loop(1, n_col)
-    def _(j):
-        pl.semaphore_signal(barrier, inc=1, device_id={"row": row, "col": lax.rem(col + j, n_col)}, device_id_type=MESH)
+    def greet(to_row, to_col):
+        pl.semaphore_signal(barrier, inc=1, device_id={"row": to_row, "col": to_col}, device_id_type=MESH)
+
+    each_other(greet)
 
     lens = jnp.broadcast_to(dl[...].astype(F32), (docs, docs))
     down = lax.broadcasted_iota(jnp.int32, (docs, docs), 0)
@@ -70,13 +80,12 @@
     starts_row = jnp.sum(jnp.where(down == along, starts_col, 0.0), axis=0, keepdims=True)
     owner_col = jnp.sum(jnp.where(down == along, dd[...].astype(F32), 0.0), axis=1, keepdims=True)
 
-    lanes = lax.broadcasted_iota(jnp.int32, (1, n_col * lot), 1)
-    shard = lax.rem(lanes, lot) // SLOTS * n_col + lanes // lot
-    first = jnp.sum(jnp.where(starts_col <= (shard * tok).astype(F32), 1.0, 0.0), axis=0, keepdims=True) - 1.0
-    slot_doc = first + lax.rem(lanes, SLOTS).astype(F32)
+    lanes = lax.broadcasted_iota(jnp.int32, (1, SLOTS * n_dev), 1)
+    first = jnp.sum(jnp.where(starts_col <= (lax.rem(lanes, n_dev) * tok).astype(F32), 1.0, 0.0), axis=0, keepdims=True) - 1.0
+    slot_doc = first + (lanes // n_dev).astype(F32)
     sel[...] = jnp.where(owner_col == slot_doc, 1.0, 0.0).astype(BF16)
 
-    base = (row * n_col + col) * tok
+    base = me * tok
     pos = base + lax.broadcasted_iota(jnp.int32, (tok, 1), 0)
     begun = (starts_row <= pos.astype(F32)) & (starts_row > jnp.full((1, 1), base, jnp.int32).astype(F32))
     slot = jnp.sum(jnp.where(begun, 1.0, 0.0), axis=1, keepdims=True)
@@ -95,32 +104,24 @@
         [jnp.where(slot == float(s), low_in, jnp.zeros_like(low_in)) for s in range(SLOTS)], axis=1
     )
     part = lax.dot_general(low_out, masked, (((0,), (0,)), ((), ())), preferred_element_type=F32)
-    for r in range(n_row):
-        for s in range(SLOTS):
-            pbuf[pl.ds(r * piece + s * n_col, n_col), :] = part[r * n_col:(r + 1) * n_col, s * rank:(s + 1) * rank]
-
-    pl.semaphore_wait(barrier, n_row + n_col - 2)
-
-    def over_row(src, dst, send, recv, j, step):
-        to = lax.rem(row + j, n_row)
-        return pltpu.make_async_remote_copy(
-            src_ref=src.at[pl.ds(to * step, step), :], dst_ref=dst.at[pl.ds(row * step, step), :],
-            send_sem=send.at[j], recv_sem=recv.at[j], device_id={"row": to, "col": col}, device_id_type=MESH,
-        )
-
-    def over_col(src, dst, send, recv, j, step, whole):
-        to = lax.rem(col + j, n_col)
-        at = col if whole else to
-        return pltpu.make_async_remote_copy(
-            src_ref=src.at[pl.ds(at * step, step), :], dst_ref=dst.at[pl.ds(col * step, step), :],
-            send_sem=send.at[j], recv_sem=recv.at[j], device_id={"row": row, "col": to}, device_id_type=MESH,
-        )
-
-    @pl.loop(1, n_row)
-    def _(j):
-        over_row(pbuf, rbuf, s1, r1, j, piece).start()
-
-    rbuf[pl.ds(row * piece, piece), :] = pbuf[pl.ds(row * piece, piece), :]
+    for s in range(SLOTS):
+        pbuf[pl.ds(s, rank, stride=PAD), :] = part[:, s * rank:(s + 1) * rank]
+
+    pl.semaphore_wait(barrier, n_dev - 1)
+
+    def slots_of(ref, i):
+        return ref.at[pl.ds(pl.multiple_of(i * PAD, PAD), SLOTS), :]
+
+    def give(to_row, to_col):
+        pltpu.make_async_remote_copy(
+            src_ref=slots_of(pbuf, to_row * n_col + to_col), dst_ref=slots_of(tbuf, me), send_sem=s1, recv_sem=r1,
+            device_id={"row": to_row, "col": to_col}, device_id_type=MESH,
+        ).start()
+
+    each_other(give)
+
+    at = pl.ds(pl.multiple_of(me * PAD, PAD), SLOTS)
+    tbuf[at, :] = pbuf[at, :]
 
     f_load.wait()
 
@@ -129,24 +130,10 @@
         at = pl.ds(pl.multiple_of(i * 32, 32), 32)
         fhi[at, :], flo[at, :] = split(f32buf[at, :])
 
-    @pl.loop(1, n_row)
-    def _(j):
-        over_row(pbuf, rbuf, s1, r1, j, piece).wait()
-
-    for c in range(n_col):
-        sbuf[pl.ds(c * lot, lot), :] = rbuf[pl.ds(c, lot, stride=n_col), :]
-
-    @pl.loop(1, n_col)
-    def _(j):
-        over_col(sbuf, tbuf, s2, r2, j, lot, False).start()
-
-    tbuf[pl.ds(col * lot, lot), :] = sbuf[pl.ds(col * lot, lot), :]
-
-    @pl.loop(1, n_col)
-    def _(j):
-        over_col(sbuf, tbuf, s2, r2, j, lot, False).wait()
-
-    t_hi, t_lo = split(tbuf[...])
+    others = pl.ds(0, (n_dev - 1) * SLOTS)
+    pltpu.make_async_copy(tbuf.at[others, :], tbuf.at[others, :], r1).wait()
+
+    t_hi, t_lo = split(jnp.concatenate([tbuf[pl.ds(s, n_dev, stride=PAD), :] for s in range(SLOTS)], axis=0))
     gbuf[col] = dot(sel[...], t_hi) + dot(sel[...], t_lo)
 
     nx = n_col // CORES
@@ -233,6 +220,7 @@
             total = total + obuf[n, j]
         out[:, n * wide:(n + 1) * wide] = total
 
+    pltpu.make_async_copy(pbuf.at[others, :], pbuf.at[others, :], s1).wait()
     for c in around + across + sum(first_hop + second_hop, []):
         c.wait_send()
 
@@ -267,10 +255,8 @@
             pltpu.VMEM((feats, cols), BF16),
             pltpu.VMEM((feats, cols), BF16),
             pltpu.VMEM((docs, slots), BF16),
-            pltpu.VMEM((slots, rank), F32),
-            pltpu.VMEM((slots, rank), F32),
-            pltpu.VMEM((slots, rank), F32),
-            pltpu.VMEM((slots, rank), F32),
+            pltpu.VMEM((n_row * n_col * PAD, rank), F32),
+            pltpu.VMEM((n_row * n_col * PAD, rank), F32),
             pltpu.VMEM((n_col, docs, rank), F32),
             pltpu.VMEM((n_col, docs, rank), BF16),
             pltpu.VMEM((n_col, docs, rank), BF16),
@@ -279,7 +265,7 @@
             pltpu.VMEM((CHUNKS, NZ, rows, cols // CHUNKS), F32),
             pltpu.VMEM((CHUNKS, NZ - 1, rows, cols // CHUNKS), F32),
             dma((n_all,)), dma((n_all,)), dma,
-            dma((n_row,)), dma((n_row,)), dma((n_col,)), dma((n_col,)),
+            dma, dma,
             dma((nx,)), dma((nx,)), dma((nx,)), dma((nx,)),
             dma((CHUNKS, NZ)), dma((CHUNKS, NZ)), dma((CHUNKS, NZ)), dma((CHUNKS, NZ)),
         ],

time: 46.5 us -> 42 us (0.903)
  Pallas kernels: 44.9 us -> 40.4 us
    pallas_call x1, Pallas kernels: 44.9 us -> 40.4 us  [per_device(): pl.pallas_call(kernel, out_shape=jax.ShapeDtypeStruct((docs // n_row, col...]
where the time goes in v3:
time: 42 us; the launch traced here: 41.8 us
  Pallas kernels  40.4 us (96%)
  local copies, waits for them, and re-layouts  1.47 us (4%)
    pallas_call x1, Pallas kernels, per_device(): pl.pallas_call(kernel, out_shape=jax.ShapeDtypeStruct((docs // n_row, col...  40.4 us
    unnamed x1, local copies, waits for them, and re-layouts  1.47 us

profile of v3, /device:TPU:1, one launch (start us, length us, event | category | flops | bytes accessed | tf_op | source)
XLA Modules:
  0.0 41.8 jit_solution(8771277358714285966)
XLA Ops:
  0.0 40.4 %shard_map.73 = f32[8,2048]{1,0:T(8,128)} custom-call(bf16[256,4096]{1,0:T(8,128)(2,1)} %refs_0_.1, bf16[256,14336]{1,0:T(8,128)(2,1)} %refs_1_.1, bf16[4096,128]{1,0:T(8,128)(2,1)} %refs_2_.1, bf16[14336,128]{1,0:T(8,128)(2,1)} %refs_3_.1, s32[1,128]{1,0:T(1,128)} %bitcast.2, s32[1,128]{1,0:T(1,128)} %bitcast.3, f32[1024,2048]{1,0:T(8,128)} %refs_6_.1), custom_call_target="tpu_custom_call" | custom-call | tf_op jit(solution)/shard_map/pallas_call | solution.py:246
  40.4 1.5 %copy.9 = f32[8,2048]{1,0:T(8,128)} copy(f32[8,2048]{1,0:T(8,128)} %shard_map.73) | data formatting | bytes 131072

commit v4 on v3

--- a/solution.py
+++ b/solution.py
@@ -245,7 +245,7 @@
 
     return pl.pallas_call(
         kernel,
-        out_shape=jax.ShapeDtypeStruct((docs // n_row, cols), F32),
+        out_shape=pltpu.VMEM((docs // n_row, cols), F32),
         in_specs=[hbm, hbm, hbm, hbm, vmem, vmem, hbm],
         out_specs=vmem,
         scratch_shapes=[

time: 42 us -> 40.5 us (0.964)
  local copies, waits for them, and re-layouts: 1.47 us -> 0.63 us
  Pallas kernels: 40.4 us -> 39.7 us
    unnamed x1, local copies, waits for them, and re-layouts: 1.47 us -> 0.63 us
    pallas_call x1, Pallas kernels: 40.4 us -> 39.7 us  [per_device(): pl.pallas_call(kernel, out_shape=pltpu.VMEM((docs // n_row, cols), F32),...]
where the time goes in v4:
time: 40.5 us; the launch traced here: 40.3 us
  Pallas kernels  39.7 us (98%)
  local copies, waits for them, and re-layouts  0.63 us (2%)
    pallas_call x1, Pallas kernels, per_device(): pl.pallas_call(kernel, out_shape=pltpu.VMEM((docs // n_row, cols), F32),...  39.7 us

profile of v4, /device:TPU:1, one launch (start us, length us, event | category | flops | bytes accessed | tf_op | source)
XLA Modules:
  0.0 40.3 jit_solution(12604363392800015133)
XLA Ops:
  0.0 39.7 %shard_map.73 = f32[8,2048]{1,0:T(8,128)S(1)} custom-call(bf16[256,4096]{1,0:T(8,128)(2,1)} %refs_0_.1, bf16[256,14336]{1,0:T(8,128)(2,1)} %refs_1_.1, bf16[4096,128]{1,0:T(8,128)(2,1)} %refs_2_.1, bf16[14336,128]{1,0:T(8,128)(2,1)} %refs_3_.1, s32[1,128]{1,0:T(1,128)} %bitcast.2, s32[1,128]{1,0:T(1,128)} %bitcast.3, f32[1024,2048]{1,0:T(8,128)} %refs_6_.1), custom_call_target="tpu_custom_call" | custom-call | tf_op jit(solution)/shard_map/pallas_call | solution.py:246
  39.7 0.6 %copy.9 = f32[8,2048]{1,0:T(8,128)} copy(f32[8,2048]{1,0:T(8,128)S(1)} %shard_map.73) | data formatting | bytes 131072

commit v5 on v4

--- a/solution.py
+++ b/solution.py
@@ -9,7 +9,9 @@
 PAD = 8
 CORES = 2
 NZ = 4
-CHUNKS = 4
+WIDTHS = (1, 1, 2, 2, 1, 1)
+CHUNKS = len(WIDTHS)
+EARLY = 2
 F32 = jnp.float32
 BF16 = jnp.bfloat16
 MESH = pl.DeviceIdType.MESH
@@ -78,12 +80,6 @@
     along = lax.broadcasted_iota(jnp.int32, (docs, docs), 1)
     starts_col = jnp.sum(jnp.where(along < down, lens, 0.0), axis=1, keepdims=True)
     starts_row = jnp.sum(jnp.where(down == along, starts_col, 0.0), axis=0, keepdims=True)
-    owner_col = jnp.sum(jnp.where(down == along, dd[...].astype(F32), 0.0), axis=1, keepdims=True)
-
-    lanes = lax.broadcasted_iota(jnp.int32, (1, SLOTS * n_dev), 1)
-    first = jnp.sum(jnp.where(starts_col <= (lax.rem(lanes, n_dev) * tok).astype(F32), 1.0, 0.0), axis=0, keepdims=True) - 1.0
-    slot_doc = first + (lanes // n_dev).astype(F32)
-    sel[...] = jnp.where(owner_col == slot_doc, 1.0, 0.0).astype(BF16)
 
     base = me * tok
     pos = base + lax.broadcasted_iota(jnp.int32, (tok, 1), 0)
@@ -123,6 +119,13 @@
     at = pl.ds(pl.multiple_of(me * PAD, PAD), SLOTS)
     tbuf[at, :] = pbuf[at, :]
 
+    owner_col = jnp.sum(jnp.where(down == along, dd[...].astype(F32), 0.0), axis=1, keepdims=True)
+
+    lanes = lax.broadcasted_iota(jnp.int32, (1, SLOTS * n_dev), 1)
+    first = jnp.sum(jnp.where(starts_col <= (lax.rem(lanes, n_dev) * tok).astype(F32), 1.0, 0.0), axis=0, keepdims=True) - 1.0
+    slot_doc = first + (lanes // n_dev).astype(F32)
+    sel[...] = jnp.where(owner_col == slot_doc, 1.0, 0.0).astype(BF16)
+
     f_load.wait()
 
     @pl.loop(0, fi.shape[0] // 32)
@@ -161,6 +164,19 @@
         across.append(hand(at, sibling, s5.at[j], r5.at[j]))
         across[j].start()
         keep(at)
+    def product(side, cols):
+        at = [x * CORES + side for x in range(nx)]
+        a_hi, a_lo = (jnp.concatenate([b[c] for c in at], axis=1) for b in (ghi, glo))
+        b_hi, b_lo = (
+            jnp.concatenate([b[pl.ds(pl.multiple_of(c * rank, rank), rank), cols] for c in at], axis=0) for b in (fhi, flo)
+        )
+        return dot(a_hi, b_hi) + (dot(a_hi, b_lo) + dot(a_lo, b_hi))
+
+    unit = ybuf.shape[3] // sum(WIDTHS)
+    begin = [unit * sum(WIDTHS[:n]) for n in range(CHUNKS + 1)]
+    for n in range(EARLY):
+        cols = slice(begin[n], begin[n + 1])
+        ybuf[:, :, :, cols] = product(core, cols).reshape(n_row // NZ, NZ, docs // n_row, begin[n + 1] - begin[n])
     for j in range(nx):
         across[j].wait_recv()
         keep(lax.rem(cx + nx - j, nx) * CORES + 1 - core)
@@ -168,7 +184,6 @@
     ny = n_row // NZ
     y, z = row // NZ, lax.rem(row, NZ)
     rows = docs // n_row
-    wide = ybuf.shape[3] // CHUNKS
     g_hi = jnp.concatenate([ghi[c] for c in range(n_col)], axis=1)
     g_lo = jnp.concatenate([glo[c] for c in range(n_col)], axis=1)
 
@@ -181,44 +196,50 @@
 
     first_hop, second_hop = [], []
     for n in range(CHUNKS):
-        cols = slice(n * wide, (n + 1) * wide)
-        f_hi, f_lo = fhi[:, cols], flo[:, cols]
-        prod = dot(g_hi, f_hi) + (dot(g_hi, f_lo) + dot(g_lo, f_hi))
-        ybuf[:, :, :, cols] = prod.reshape(ny, NZ, rows, wide)
+        cols = slice(begin[n], begin[n + 1])
+        wide = begin[n + 1] - begin[n]
+        if n < EARLY:
+            ybuf[:, :, :, cols] += product(1 - core, cols).reshape(ny, NZ, rows, wide)
+        else:
+            f_hi, f_lo = fhi[:, cols], flo[:, cols]
+            prod = dot(g_hi, f_hi) + (dot(g_hi, f_lo) + dot(g_lo, f_hi))
+            ybuf[:, :, :, cols] = prod.reshape(ny, NZ, rows, wide)
         hops = []
         for j in range(1, ny if n % 2 == 0 else NZ):
             to, device = peer(n % 2 == 0, j)
             src = ybuf.at[to, :, :, cols] if n % 2 == 0 else ybuf.at[:, to, :, cols]
             hops.append(pltpu.make_async_remote_copy(
-                src_ref=src, dst_ref=mbuf.at[n, j - 1], send_sem=s4.at[n, j], recv_sem=r4.at[n, j],
+                src_ref=src, dst_ref=mbuf.at[n, j - 1, :, :, 0:wide], send_sem=s4.at[n, j], recv_sem=r4.at[n, j],
                 device_id=device, device_id_type=MESH,
             ))
             hops[-1].start()
         first_hop.append(hops)
 
     for n in range(CHUNKS):
-        cols = slice(n * wide, (n + 1) * wide)
+        cols = slice(begin[n], begin[n + 1])
+        wide = begin[n + 1] - begin[n]
         part = ybuf[y, :, :, cols] if n % 2 == 0 else ybuf[:, z, :, cols]
         for j, c in enumerate(first_hop[n]):
             c.wait_recv()
-            part = part + mbuf[n, j]
-        qbuf[n] = part
+            part = part + mbuf[n, j, :, :, 0:wide]
+        qbuf[n, :, :, 0:wide] = part
         hops = []
         for j in range(1, NZ if n % 2 == 0 else ny):
             to, device = peer(n % 2 == 1, j)
             hops.append(pltpu.make_async_remote_copy(
-                src_ref=qbuf.at[n, to], dst_ref=obuf.at[n, j - 1], send_sem=s6.at[n, j], recv_sem=r6.at[n, j],
+                src_ref=qbuf.at[n, to, :, 0:wide], dst_ref=obuf.at[n, j - 1, :, 0:wide], send_sem=s6.at[n, j], recv_sem=r6.at[n, j],
                 device_id=device, device_id_type=MESH,
             ))
             hops[-1].start()
         second_hop.append(hops)
 
     for n in range(CHUNKS):
-        total = qbuf[n, z if n % 2 == 0 else y]
+        wide = begin[n + 1] - begin[n]
+        total = qbuf[n, z if n % 2 == 0 else y, :, 0:wide]
         for j, c in enumerate(second_hop[n]):
             c.wait_recv()
-            total = total + obuf[n, j]
-        out[:, n * wide:(n + 1) * wide] = total
+            total = total + obuf[n, j, :, 0:wide]
+        out[:, begin[n]:begin[n + 1]] = total
 
     pltpu.make_async_copy(pbuf.at[others, :], pbuf.at[others, :], s1).wait()
     for c in around + across + sum(first_hop + second_hop, []):
@@ -261,9 +282,9 @@
             pltpu.VMEM((n_col, docs, rank), BF16),
             pltpu.VMEM((n_col, docs, rank), BF16),
             pltpu.VMEM((ny, NZ, rows, cols), F32),
-            pltpu.VMEM((CHUNKS, NZ - 1, NZ, rows, cols // CHUNKS), F32),
-            pltpu.VMEM((CHUNKS, NZ, rows, cols // CHUNKS), F32),
-            pltpu.VMEM((CHUNKS, NZ - 1, rows, cols // CHUNKS), F32),
+            pltpu.VMEM((CHUNKS, NZ - 1, NZ, rows, cols * max(WIDTHS) // sum(WIDTHS)), F32),
+            pltpu.VMEM((CHUNKS, NZ, rows, cols * max(WIDTHS) // sum(WIDTHS)), F32),
+            pltpu.VMEM((CHUNKS, NZ - 1, rows, cols * max(WIDTHS) // sum(WIDTHS)), F32),
             dma((n_all,)), dma((n_all,)), dma,
             dma, dma,
             dma((nx,)), dma((nx,)), dma((nx,)), dma((nx,)),

time: 40.5 us -> 40.3 us (level)
  no operation moved by 1% of the time
where the time goes in v5:
time: 40.3 us; the launch traced here: 40.2 us
  Pallas kernels  39.6 us (98%)
  local copies, waits for them, and re-layouts  0.63 us (2%)
    pallas_call x1, Pallas kernels, per_device(): pl.pallas_call(kernel, out_shape=pltpu.VMEM((docs // n_row, cols), F32),...  39.6 us

profile of v5, /device:TPU:1, one launch (start us, length us, event | category | flops | bytes accessed | tf_op | source)
XLA Modules:
  0.0 40.2 jit_solution(8838853072950292889)
XLA Ops:
  0.0 39.6 %shard_map.73 = f32[8,2048]{1,0:T(8,128)S(1)} custom-call(bf16[256,4096]{1,0:T(8,128)(2,1)} %refs_0_.1, bf16[256,14336]{1,0:T(8,128)(2,1)} %refs_1_.1, bf16[4096,128]{1,0:T(8,128)(2,1)} %refs_2_.1, bf16[14336,128]{1,0:T(8,128)(2,1)} %refs_3_.1, s32[1,128]{1,0:T(1,128)} %bitcast.2, s32[1,128]{1,0:T(1,128)} %bitcast.3, f32[1024,2048]{1,0:T(8,128)} %refs_6_.1), custom_call_target="tpu_custom_call" | custom-call | tf_op jit(solution)/shard_map/pallas_call | solution.py:267
  39.6 0.6 %copy.9 = f32[8,2048]{1,0:T(8,128)} copy(f32[8,2048]{1,0:T(8,128)S(1)} %shard_map.73) | data formatting | bytes 131072

commit v6 on v5

--- a/solution.py
+++ b/solution.py
@@ -66,7 +66,6 @@
         for c in loads[-1]:
             c.start()
     f_load = pltpu.make_async_copy(fi, f32buf, f_sem)
-    f_load.start()
 
     barrier = pltpu.get_barrier_semaphore()
 
@@ -114,6 +113,7 @@
             device_id={"row": to_row, "col": to_col}, device_id_type=MESH,
         ).start()
 
+    f_load.start()
     each_other(give)
 
     at = pl.ds(pl.multiple_of(me * PAD, PAD), SLOTS)

time: 40.3 us -> 40.4 us (level)
  no operation moved by 1% of the time
where the time goes in v6:
time: 40.4 us; the launch traced here: 40.2 us
  Pallas kernels  39.6 us (98%)
  local copies, waits for them, and re-layouts  0.63 us (2%)
    pallas_call x1, Pallas kernels, per_device(): pl.pallas_call(kernel, out_shape=pltpu.VMEM((docs // n_row, cols), F32),...  39.6 us

profile of v6, /device:TPU:1, one launch (start us, length us, event | category | flops | bytes accessed | tf_op | source)
XLA Modules:
  0.0 40.2 jit_solution(4692195119099531534)
XLA Ops:
  0.0 39.6 %shard_map.73 = f32[8,2048]{1,0:T(8,128)S(1)} custom-call(bf16[256,4096]{1,0:T(8,128)(2,1)} %refs_0_.1, bf16[256,14336]{1,0:T(8,128)(2,1)} %refs_1_.1, bf16[4096,128]{1,0:T(8,128)(2,1)} %refs_2_.1, bf16[14336,128]{1,0:T(8,128)(2,1)} %refs_3_.1, s32[1,128]{1,0:T(1,128)} %bitcast.2, s32[1,128]{1,0:T(1,128)} %bitcast.3, f32[1024,2048]{1,0:T(8,128)} %refs_6_.1), custom_call_target="tpu_custom_call" | custom-call | tf_op jit(solution)/shard_map/pallas_call | solution.py:267
  39.6 0.6 %copy.9 = f32[8,2048]{1,0:T(8,128)} copy(f32[8,2048]{1,0:T(8,128)S(1)} %shard_map.73) | data formatting | bytes 131072
